TPU v7x, 32 devices: a whole 2x2x4 slice. The times are simulated.
32 devices in a mesh: groups: 2 (over y), fsdp: 8 (over z, x), seq: 2 (over core).
Axes of the slice: x: 2, y: 2, z: 4, core: 2. Of those that a mesh axis runs over, the one named last changes fastest.
Arguments:
- tokens: bfloat16 [2048, 8192], P(('groups', 'fsdp', 'seq')), parts along dimension 0, may hold values from -6 to 6
- gate_blocks: bfloat16 [1280, 4096], P('fsdp'), may hold values from -0.09375 to 0.09375
- gate_slot: int32 [1280], P('fsdp'), may hold values from 0 to 256, as said below
- up_blocks: bfloat16 [1280, 4096], P('fsdp'), may hold values from -0.09375 to 0.09375
- up_slot: int32 [1280], P('fsdp'), may hold values from 0 to 256, as said below
- down_blocks: bfloat16 [1280, 4096], P('fsdp'), may hold values from -0.25 to 0.25
- down_slot: int32 [1280], P('fsdp'), may hold values from 0 to 256, as said below
- sketch: bfloat16 [32, 8192], P(None, 'fsdp'), may hold values from -0.0625 to 0.0625
- probe_index: int32 [16, 256], replicated, may hold values from 0 to 8191
- probe_value: float32 [16, 256], replicated, may hold values from -32 to 32
Outputs:
- products: float32 [32, 8192], P('groups', 'fsdp'), parts along dimension 0
There are 2 independent parts, one for each index of `groups`. A program takes and returns all parts, laid end to end along the dimension named above; an argument that names none is the same for every part. Nothing has to cross between parts.
Inputs may be any that keep to these rules, and one draw needn't show every extreme that they name: `gate_slot`: slots j * 160 to (j + 1) * 160 - 1 belong to fsdp owner j; they hold distinct block numbers below 256, filled slots first, then the value 256 for empty slots. Every owner fills 3 * 32 slots or more, and in every draw some owner fills all 160. `up_slot`: as for gate_slot, drawn independently. `down_slot`: as for gate_slot, drawn independently.
All inputs are finite; a program needn't handle non-finite values.
Results may differ from a plain program's by a relative error of at most 0.0038.
Values may be sent and summed in bfloat16 or wider, within the bound.
No kernel may reach another device: no remote copies, remote signals or barrier semaphores. Data moves between devices by JAX's collectives and lax.ppermute only.
A program may use at most 128 MiB of HBM per device.

v0:
```python
import jax
import jax.numpy as jnp
from jax import lax
from jax.sharding import PartitionSpec as P

HID_DEV = 128
BLK = 64
P_SIZE = 16
K = 32


def unpack(blocks, slot_ids, cell_total):
    holder = jnp.zeros((cell_total + 1, blocks.shape[1]), blocks.dtype)
    return holder.at[slot_ids].set(blocks)[:cell_total]


def contract_last(first_mat, second_mat):
    return lax.dot_general(
        first_mat, second_mat, (((1,), (1,)), ((), ())), preferred_element_type=jnp.float32
    )


def per_device(
    tokens,
    gate_blocks,
    gate_slot,
    up_blocks,
    up_slot,
    down_blocks,
    down_slot,
    sketch,
    probe_index,
    probe_value,
):
    owners = lax.axis_size("fsdp")
    model_width = tokens.shape[1]
    local_width = model_width // owners
    block_rows = local_width // BLK
    hidden = HID_DEV
    col_blocks = hidden * owners // BLK
    cell_total = block_rows * col_blocks
    gate_dense = unpack(gate_blocks, gate_slot, cell_total).reshape(
        block_rows, col_blocks, BLK, BLK
    )
    up_dense = unpack(up_blocks, up_slot, cell_total).reshape(block_rows, col_blocks, BLK, BLK)
    stacked = jnp.stack([gate_dense, up_dense], axis=1)
    stacked = stacked.reshape(block_rows, 2, owners, hidden // BLK, BLK, BLK)
    stacked = stacked.transpose(0, 4, 2, 1, 3, 5).reshape(local_width, owners * 2 * hidden)
    both_weights = lax.all_to_all(stacked, "fsdp", split_axis=1, concat_axis=0, tiled=True)
    picked = both_weights[probe_index].astype(jnp.float32)
    probe_both = jnp.sum(picked * probe_value[:, :, None], axis=1)
    preact = jnp.dot(
        lax.all_gather(tokens, "fsdp", axis=0, tiled=True),
        both_weights,
        preferred_element_type=jnp.float32,
    )
    row_count = preact.shape[0]
    gate_pre = preact[:, :hidden]
    up_pre = preact[:, hidden:]
    down_dense = unpack(down_blocks, down_slot, cell_total).reshape(
        col_blocks, block_rows, BLK, BLK
    )
    down_dense = down_dense.transpose(0, 2, 1, 3).reshape(col_blocks * BLK, local_width)
    down_rows = lax.all_to_all(down_dense, "fsdp", split_axis=0, concat_axis=1, tiled=True)
    full_sketch = lax.all_gather(sketch, "fsdp", axis=1, tiled=True)
    projected = contract_last(down_rows, full_sketch)
    projected = projected.astype(jnp.bfloat16)
    sigmoid_g = jax.nn.sigmoid(gate_pre)
    activated = gate_pre * sigmoid_g
    slope_g = sigmoid_g * (1.0 + gate_pre * (1.0 - sigmoid_g))
    lead_term = slope_g * up_pre
    tangent = (
        lead_term[:, None, :] * probe_both[None, :, :hidden]
        + activated[:, None, :] * probe_both[None, :, hidden:]
    )
    tangent = tangent.astype(jnp.bfloat16)
    partial_sketch = jnp.dot(
        tangent.reshape(row_count * P_SIZE, hidden), projected, preferred_element_type=jnp.float32
    )
    partial_sketch = partial_sketch.reshape(row_count, P_SIZE * K)
    sketch_rows = lax.psum(partial_sketch, "fsdp").astype(jnp.bfloat16)
    backward = contract_last(sketch_rows.reshape(row_count * P_SIZE, K), projected).reshape(
        row_count, P_SIZE, hidden
    )
    summed = jnp.concatenate(
        [
            jnp.sum(backward * lead_term[:, None, :], axis=0),
            jnp.sum(backward * activated[:, None, :], axis=0),
        ],
        axis=1,
    )
    summed = lax.psum(summed, "seq").astype(jnp.bfloat16)
    products = contract_last(summed, both_weights)
    return lax.psum_scatter(products, "fsdp", scatter_dimension=1, tiled=True)


def solution(mesh):
    in_specs = (
        P(("groups", "fsdp", "seq"), None),
        P("fsdp", None),
        P("fsdp"),
        P("fsdp", None),
        P("fsdp"),
        P("fsdp", None),
        P("fsdp"),
        P(None, "fsdp"),
        P(),
        P(),
    )
    out_specs = P("groups", "fsdp")
    return jax.shard_map(
        per_device, mesh=mesh, in_specs=in_specs, out_specs=out_specs, check_vma=False
    )
```

profile of v0, /device:TPU:0, one launch (start us, length us, event | category | flops | bytes accessed | tf_op | source)
XLA Modules:
  0.0 471.8 jit_solution(3671803869858965092)
XLA Ops:
  7.9 3.9 scatter_custom_fusion.2
  13.3 6.9 %reshape.39 = bf16[16,16,64,64]{3,2,1,0:T(8,128)(2,1)} reshape(bf16[256,4096]{1,0:T(8,128)(2,1)} %slice.36) | data formatting | bytes 4194304 | tf_op jit(solution)/shard_map/reshape | solution.py:60
  20.2 8.0 %copy.32 = bf16[16,16,64,64]{3,1,2,0:T(8,128)(2,1)} copy(bf16[16,16,64,64]{3,2,1,0:T(8,128)(2,1)} %reshape.39) | data formatting | bytes 4194304 | tf_op jit(solution)/shard_map/reshape | solution.py:60
  28.2 6.5 %all_to_all.32 = bf16[8,128,1024]{2,1,0:T(8,128)(2,1)} reshape(bf16[16,64,16,64]{3,2,1,0:T(8,128)(2,1)} %bitcast.42) | data formatting | bytes 4194304 | tf_op jit(solution)/shard_map/all_to_all | solution.py:64
  34.8 7.3 %all-to-all-start.1 = ((bf16[8,128,1024]{2,1,0:T(8,128)(2,1)}), bf16[8,128,1024]{2,1,0:T(8,128)(2,1)}, u32[]{:S(2)}, u32[]{:S(2)}) async-start(bf16[8,128,1024]{2,1,0:T(8,128)(2,1)} %all_to_all.32), calls=%async_computation.1 | async-start | bytes 4194304 | tf_op jit(solution)/shard_map/all_to_all | solution.py:64
  42.0 4.0 scatter_custom_fusion
  47.6 6.9 %stack.7 = bf16[16,1,8,2,64,64]{5,4,3,2,0,1:T(8,128)(2,1)} reshape(bf16[256,4096]{1,0:T(8,128)(2,1)} %slice.30) | data formatting | bytes 4194304 | tf_op jit(solution)/shard_map/stack | solution.py:46
  54.5 3.9 scatter_custom_fusion.1
  59.9 6.9 %stack.8 = bf16[16,1,8,2,64,64]{5,4,3,2,0,1:T(8,128)(2,1)} reshape(bf16[256,4096]{1,0:T(8,128)(2,1)} %slice.31) | data formatting | bytes 4194304 | tf_op jit(solution)/shard_map/stack | solution.py:46
  66.7 8.6 %maximum_bitcast_fusion = bf16[16,64,8,2,2,64]{5,1,4,2,0,3:T(8,128)(2,1)} fusion(bf16[16,1,8,2,64,64]{5,4,3,2,0,1:T(8,128)(2,1)} %stack.8, bf16[16,1,8,2,64,64]{5,4,3,2,0,1:T(8,128)(2,1)} %stack.7), kind=kLoop, calls=%fused_computation.4 | loop fusion | flops 2097152 | bytes 8388608 | tf_op jit(solution)/shard_map/transpose | solution.py:48
  75.3 13.1 %copy.20 = bf16[16,64,8,2,2,64]{1,0,5,4,3,2:T(8,128)(2,1)} copy(bf16[16,64,8,2,2,64]{5,1,4,2,0,3:T(8,128)(2,1)} %maximum_bitcast_fusion) | data formatting | bytes 8388608 | tf_op jit(solution)/shard_map/transpose | solution.py:48
  88.4 12.0 %all_to_all.28 = bf16[1024,8,256]{0,2,1:T(8,128)(2,1)} reshape(bf16[16,64,8,2,2,64]{1,0,5,4,3,2:T(8,128)(2,1)} %copy.20) | data formatting | bytes 8388608 | tf_op jit(solution)/shard_map/all_to_all | solution.py:49
  100.4 34.2 %all-to-all-done.1 = bf16[8,128,1024]{2,1,0:T(8,128)(2,1)} async-done(((bf16[8,128,1024]{2,1,0:T(8,128)(2,1)}), bf16[8,128,1024]{2,1,0:T(8,128)(2,1)}, u32[]{:S(2)}, u32[]{:S(2)}) %all-to-all-start.1) | async-done | bytes 2097184 | tf_op jit(solution)/shard_map/all_to_all | solution.py:64
  134.5 5.9 %all-to-all-start = ((bf16[1024,8,256]{0,2,1:T(8,128)(2,1)}), bf16[1024,8,256]{0,2,1:T(8,128)(2,1)}, u32[]{:S(2)}, u32[]{:S(2)}) async-start(bf16[1024,8,256]{0,2,1:T(8,128)(2,1)} %all_to_all.28), calls=%async_computation | async-start | bytes 8388608 | tf_op jit(solution)/shard_map/all_to_all | solution.py:49
  140.5 141.7 %all_gather.7 = bf16[32,8192]{1,0:T(8,128)(2,1)S(1)} all-gather(bf16[32,1024]{1,0:T(8,128)(2,1)S(1)} %copy-done), channel_id=1, replica_groups=mesh['groups'=2,'fsdp'=8,'seq'=2] {'fsdp'}, dimensions={1}, use_global_device_ids=true | all-gather | bytes 589824 | tf_op jit(solution)/shard_map/all_gather | solution.py:65
  282.2 3.0 copy.26
  285.7 6.5 %copy.21 = bf16[8,1024,256]{2,1,0:T(8,128)(2,1)} copy(bf16[8,1024,256]{1,2,0:T(8,128)(2,1)} %bitcast.1) | data formatting | bytes 8388608 | tf_op jit(solution)/shard_map/all_to_all | solution.py:49
  292.2 15.7 %gather_fusion = bf16[4096,256]{1,0:T(8,128)(2,1)S(1)} fusion(bf16[8192,256]{1,0:T(8,128)(2,1)} %bitcast.39, s32[4096]{0:T(1024)S(1)} %broadcast_clamp_fusion), kind=kCustom, calls=%fused_computation | custom fusion | bytes 4210688 | tf_op jit(solution)/shard_map/gather | solution.py:50
  308.7 7.0 %convolution_bitcast_fusion = f32[512,256]{0,1:T(8,128)S(1)} fusion(bf16[8192,256]{1,0:T(8,128)(2,1)} %bitcast.40, bf16[512,8192]{1,0:T(8,128)(2,1)} %all-gather.2.cloned.1.call-done), kind=kOutput, calls=%fused_computation.11 | convolution fusion | flops 2147483648 | bytes 13107200 | tf_op jit(solution)/shard_map/dot_general | solution.py:52
  320.7 3.5 reshape.40
  324.2 70.7 %all-reduce.1 = bf16[512,512]{1,0:T(8,128)(2,1)S(1)} all-reduce(f32[512,512]{1,0:T(8,128)S(1)} %reshape.40), channel_id=1, replica_groups=mesh['groups'=2,'fsdp'=8,'seq'=2] {'fsdp'}, use_global_device_ids=true, to_apply=%region_4.0 | all-reduce | flops 262144 | bytes 1572864 | tf_op jit(solution)/shard_map/psum | solution.py:81
  396.2 3.4 psum.15
  399.6 4.2 fusion.15
  403.8 61.1 %reduce-scatter.2.cloned.1.call-done = f32[16,1024]{1,0:T(8,128)} async-done(((f32[16,8192]{1,0:T(8,128)}), f32[16,1024]{1,0:T(8,128)}) %reduce-scatter.2.cloned.1.call-update) | async-done | bytes 65552 | tf_op jit(solution)/shard_map/reduce_scatter | solution.py:94
  (37 shorter events, 13.2 us)
Async XLA Ops:
  6.5 302.2 %all-gather.2.cloned.1.call-start = ((), (), s32[]{:S(2)}) async-start(), calls=%async_computation.3 | async-start | bytes 9437184 | tf_op jit(solution)/shard_map/all_gather | solution.py:53
  34.8 7.3 %copy-start.3 = (s32[160]{0:T(256)S(1)}, s32[160]{0:T(256)}, u32[]{:S(2)}) copy-start(s32[160]{0:T(256)} %param.12) | copy-start | bytes 1924
  34.8 99.8 %all-to-all-start.1 = ((bf16[8,128,1024]{2,1,0:T(8,128)(2,1)}), bf16[8,128,1024]{2,1,0:T(8,128)(2,1)}, u32[]{:S(2)}, u32[]{:S(2)}) async-start(bf16[8,128,1024]{2,1,0:T(8,128)(2,1)} %all_to_all.32), calls=%async_computation.1 | async-start | bytes 4194304 | tf_op jit(solution)/shard_map/all_to_all | solution.py:64
  47.6 6.9 %copy-start.4 = (s32[160]{0:T(256)S(1)}, s32[160]{0:T(256)}, u32[]{:S(2)}) copy-start(s32[160]{0:T(256)} %param.14) | copy-start | bytes 1924
  100.4 40.1 %copy-start.2 = (s32[16,256]{1,0:T(8,128)S(1)}, s32[16,256]{1,0:T(8,128)}, u32[]{:S(2)}) copy-start(s32[16,256]{1,0:T(8,128)} %param.18) | copy-start | bytes 49156
  100.4 40.2 %copy-start = (bf16[32,1024]{1,0:T(8,128)(2,1)S(1)}, bf16[32,1024]{1,0:T(8,128)(2,1)}, u32[]{:S(2)}) copy-start(bf16[32,1024]{1,0:T(8,128)(2,1)} %param.17) | copy-start | bytes 196612
  134.5 151.2 %all-to-all-start = ((bf16[1024,8,256]{0,2,1:T(8,128)(2,1)}), bf16[1024,8,256]{0,2,1:T(8,128)(2,1)}, u32[]{:S(2)}, u32[]{:S(2)}) async-start(bf16[1024,8,256]{0,2,1:T(8,128)(2,1)} %all_to_all.28), calls=%async_computation | async-start | bytes 8388608 | tf_op jit(solution)/shard_map/all_to_all | solution.py:49
  140.4 324.5 %reduce-scatter.2.cloned.1.call-start = ((), (), s32[]{:S(2)}) async-start(), calls=%async_computation.4 | async-start | bytes 589824 | tf_op jit(solution)/shard_map/reduce_scatter | solution.py:94
  292.2 15.7 %copy-start.1 = (f32[16,256]{1,0:T(8,128)S(1)}, f32[16,256]{1,0:T(8,128)}, u32[]{:S(2)}) copy-start(f32[16,256]{1,0:T(8,128)} %param.19) | copy-start | bytes 49156
Sparse Core Ops, SparseCore 0:
  9.5 226.6 all-gather.1
  403.9 60.9 reduce-scatter.1
where the time goes:
time: 474 us; the launch traced here: 472 us
  blocking collectives  216 us (46%)
  local copies, waits for them, and re-layouts  107 us (23%)
  waiting for transfers between devices  96 us (20%)
  matrix products  15.2 us (3%)
  between operations  13.6 us (3%)
  starting transfers between devices  13.2 us (3%)
  other arithmetic  10.7 us (2%)
    all_gather x1, blocking collectives, per_device(): full_sketch = lax.all_gather(sketch, 'fsdp', axis=1, tiled=True)  142 us
    psum x1, blocking collectives, per_device(): sketch_rows = lax.psum(partial_sketch, 'fsdp').astype(jnp.bfloat16)  70.7 us
    reduce_scatter x1, waiting for transfers between devices, per_device(): return lax.psum_scatter(products, 'fsdp', scatter_dimension=1, tiled=True)  61.1 us
    all_to_all x1, waiting for transfers between devices, per_device(): lax.all_to_all(down_dense, 'fsdp', split_axis=0, concat_axis=1, tiled=True)  34.2 us
    all_to_all x2, local copies, waits for them, and re-layouts, per_device(): lax.all_to_all(stacked, 'fsdp', split_axis=1, concat_axis=0, tiled=True)  18.5 us
    gather x1, local copies, waits for them, and re-layouts, per_device(): picked = both_weights[probe_index].astype(jnp.float32)  15.7 us
    reshape x2, local copies, waits for them, and re-layouts, per_device(): unpack(down_blocks, down_slot, cell_total)  14.9 us
    another operation x2, local copies, waits for them, and re-layouts, per_device(): stacked = jnp.stack([gate_dense, up_dense], axis=1)  13.8 us
  transfers between devices with their start and end apart: 4, of which 2 were waited for; matrix products, arithmetic and copies ran while one was open for 20% of the time, Pallas kernels for 0%

commit v1 on v0

--- a/solution.py
+++ b/solution.py
@@ -7,6 +7,22 @@
 BLK = 64
 P_SIZE = 16
 K = 32
+
+
+def exchange_in_pairs(x, axis, split, join):
+    ways, here = (lax.axis_size(axis), lax.axis_index(axis))
+    width = x.shape[split] // ways
+    shape = list(x.shape)
+    shape[split] = width
+    height = shape[join]
+    shape[join] = height * ways
+    full = jnp.zeros(shape, x.dtype)
+    for mask in range(ways):
+        part = lax.dynamic_slice_in_dim(x, (here ^ mask) * width, width, axis=split)
+        if mask:
+            part = lax.ppermute(part, axis, [(d, d ^ mask) for d in range(ways)])
+        full = lax.dynamic_update_slice_in_dim(full, part, (here ^ mask) * height, axis=join)
+    return full
 
 
 def unpack(blocks, slot_ids, cell_total):
@@ -61,7 +77,7 @@
         col_blocks, block_rows, BLK, BLK
     )
     down_dense = down_dense.transpose(0, 2, 1, 3).reshape(col_blocks * BLK, local_width)
-    down_rows = lax.all_to_all(down_dense, "fsdp", split_axis=0, concat_axis=1, tiled=True)
+    down_rows = exchange_in_pairs(down_dense, "fsdp", 0, 1)
     full_sketch = lax.all_gather(sketch, "fsdp", axis=1, tiled=True)
     projected = contract_last(down_rows, full_sketch)
     projected = projected.astype(jnp.bfloat16)

time: 474 us -> 480 us (1.013)
  waiting for transfers between devices: 96 us -> 67.9 us
  blocking collectives: 216 us -> 242 us
    all_to_all x1 -> x0, waiting for transfers between devices: 34.2 us -> none  [per_device(): lax.all_to_all(down_dense, 'fsdp', split_axis=0, concat_axis=1, tiled=True)]
    all_gather x1, blocking collectives: 142 us -> 161 us  [per_device(): full_sketch = lax.all_gather(sketch, 'fsdp', axis=1, tiled=True)]
    all_to_all x2 -> x0, local copies, waits for them, and re-layouts: 9.57 us -> none  [per_device(): lax.all_to_all(down_dense, 'fsdp', split_axis=0, concat_axis=1, tiled=True)]
    ppermute x0 -> x7, starting transfers between devices: none -> 8.98 us  [exchange_in_pairs(): part = lax.ppermute(part, axis, [(d, d ^ mask) for d in range(ways)])]
    all_to_all x1 -> x0, starting transfers between devices: 7.26 us -> none  [per_device(): lax.all_to_all(down_dense, 'fsdp', split_axis=0, concat_axis=1, tiled=True)]
    psum x1, blocking collectives: 70.7 us -> 77.4 us  [per_device(): sketch_rows = lax.psum(partial_sketch, 'fsdp').astype(jnp.bfloat16)]
    reshape x0 -> x1, local copies, waits for them, and re-layouts: none -> 5.47 us  [per_device(): down_dense.transpose(0, 2, 1, 3).reshape(col_blocks * BLK, local_width)]
    dynamic_update_slice x0 -> x7, local copies, waits for them, and re-layouts: none -> 5.16 us  [exchange_in_pairs(): lax.dynamic_update_slice_in_dim(full, part, (here ^ mask) * height, axis=...]
  transfers between devices with their start and end apart: 4 -> 10, of which waited for: 2 -> 3; matrix products, arithmetic and copies ran while one was open for 20% -> 22% of each run, Pallas kernels for 0% -> 0%
where the time goes in v1:
time: 480 us; the launch traced here: 478 us
  blocking collectives  242 us (50%)
  local copies, waits for them, and re-layouts  110 us (23%)
  waiting for transfers between devices  67.9 us (14%)
  matrix products  17.2 us (4%)
  starting transfers between devices  16.6 us (3%)
  between operations  13.8 us (3%)
  other arithmetic  10.7 us (2%)
    all_gather x1, blocking collectives, per_device(): full_sketch = lax.all_gather(sketch, 'fsdp', axis=1, tiled=True)  161 us
    psum x1, blocking collectives, per_device(): sketch_rows = lax.psum(partial_sketch, 'fsdp').astype(jnp.bfloat16)  77.4 us
    reduce_scatter x1, waiting for transfers between devices, per_device(): return lax.psum_scatter(products, 'fsdp', scatter_dimension=1, tiled=True)  62.2 us
    all_to_all x2, local copies, waits for them, and re-layouts, per_device(): lax.all_to_all(stacked, 'fsdp', split_axis=1, concat_axis=0, tiled=True)  18.5 us
    gather x1, local copies, waits for them, and re-layouts, per_device(): picked = both_weights[probe_index].astype(jnp.float32)  15.7 us
    reshape x2, local copies, waits for them, and re-layouts, per_device(): unpack(down_blocks, down_slot, cell_total)  14.5 us
    another operation x2, local copies, waits for them, and re-layouts, per_device(): stacked = jnp.stack([gate_dense, up_dense], axis=1)  13.8 us
    transpose x1, local copies, waits for them, and re-layouts, per_device(): stacked.transpose(0, 4, 2, 1, 3, 5)  13.1 us
  transfers between devices with their start and end apart: 10, of which 3 were waited for; matrix products, arithmetic and copies ran while one was open for 22% of the time, Pallas kernels for 0%

profile of v1, /device:TPU:0, one launch (start us, length us, event | category | flops | bytes accessed | tf_op | source)
XLA Modules:
  0.0 478.2 jit_solution(10256307978967145144)
XLA Ops:
  8.0 3.9 scatter_custom_fusion.1
  13.3 6.9 %stack.8 = bf16[16,1,8,2,64,64]{5,4,3,2,0,1:T(8,128)(2,1)} reshape(bf16[256,4096]{1,0:T(8,128)(2,1)} %slice.31) | data formatting | bytes 4194304 | tf_op jit(solution)/shard_map/stack | solution.py:62
  20.2 3.9 scatter_custom_fusion
  25.7 6.9 %stack.7 = bf16[16,1,8,2,64,64]{5,4,3,2,0,1:T(8,128)(2,1)} reshape(bf16[256,4096]{1,0:T(8,128)(2,1)} %slice.30) | data formatting | bytes 4194304 | tf_op jit(solution)/shard_map/stack | solution.py:62
  32.6 8.6 %maximum_bitcast_fusion = bf16[16,64,8,2,2,64]{5,1,4,2,0,3:T(8,128)(2,1)} fusion(bf16[16,1,8,2,64,64]{5,4,3,2,0,1:T(8,128)(2,1)} %stack.8, bf16[16,1,8,2,64,64]{5,4,3,2,0,1:T(8,128)(2,1)} %stack.7), kind=kLoop, calls=%fused_computation.4 | loop fusion | flops 2097152 | bytes 8388608 | tf_op jit(solution)/shard_map/transpose | solution.py:64
  41.2 13.1 %copy.19 = bf16[16,64,8,2,2,64]{1,0,5,4,3,2:T(8,128)(2,1)} copy(bf16[16,64,8,2,2,64]{5,1,4,2,0,3:T(8,128)(2,1)} %maximum_bitcast_fusion) | data formatting | bytes 8388608 | tf_op jit(solution)/shard_map/transpose | solution.py:64
  54.3 12.0 %all_to_all.14 = bf16[1024,8,256]{0,2,1:T(8,128)(2,1)} reshape(bf16[16,64,8,2,2,64]{1,0,5,4,3,2:T(8,128)(2,1)} %copy.19) | data formatting | bytes 8388608 | tf_op jit(solution)/shard_map/all_to_all | solution.py:65
  66.3 7.6 %all-to-all-start = ((bf16[1024,8,256]{0,2,1:T(8,128)(2,1)}), bf16[1024,8,256]{0,2,1:T(8,128)(2,1)}, u32[]{:S(2)}, u32[]{:S(2)}) async-start(bf16[1024,8,256]{0,2,1:T(8,128)(2,1)} %all_to_all.14), calls=%async_computation | async-start | bytes 8388608 | tf_op jit(solution)/shard_map/all_to_all | solution.py:65
  73.9 3.9 scatter_custom_fusion.2
  79.2 6.9 %reshape.37 = bf16[16,16,64,64]{3,2,1,0:T(8,128)(2,1)} reshape(bf16[256,4096]{1,0:T(8,128)(2,1)} %slice.36) | data formatting | bytes 4194304 | tf_op jit(solution)/shard_map/reshape | solution.py:76
  86.1 7.7 %copy.30 = bf16[16,16,64,64]{3,1,2,0:T(8,128)(2,1)} copy(bf16[16,16,64,64]{3,2,1,0:T(8,128)(2,1)} %reshape.37) | data formatting | bytes 4194304 | tf_op jit(solution)/shard_map/reshape | solution.py:76
  93.8 5.5 %reshape.38 = bf16[1024,1024]{1,0:T(8,128)(2,1)S(1)} reshape(bf16[16,64,16,64]{3,2,1,0:T(8,128)(2,1)} %bitcast.40) | data formatting | bytes 4194304 | tf_op jit(solution)/shard_map/reshape | solution.py:79
  105.4 2.8 collective-permute-start.3
  109.7 161.0 %all_gather.7 = bf16[32,8192]{1,0:T(8,128)(2,1)S(1)} all-gather(bf16[32,1024]{1,0:T(8,128)(2,1)S(1)} %copy-done.1), channel_id=1, replica_groups=mesh['groups'=2,'fsdp'=8,'seq'=2] {'fsdp'}, dimensions={1}, use_global_device_ids=true | all-gather | bytes 589824 | tf_op jit(solution)/shard_map/all_gather | solution.py:81
  275.7 3.3 collective-permute-done.5
  284.4 6.5 %copy.20 = bf16[8,1024,256]{2,1,0:T(8,128)(2,1)} copy(bf16[8,1024,256]{1,2,0:T(8,128)(2,1)} %bitcast.1) | data formatting | bytes 8388608 | tf_op jit(solution)/shard_map/all_to_all | solution.py:65
  290.9 15.7 %gather_fusion = bf16[4096,256]{1,0:T(8,128)(2,1)S(1)} fusion(bf16[8192,256]{1,0:T(8,128)(2,1)} %bitcast.37, s32[4096]{0:T(1024)S(1)} %broadcast_clamp_fusion), kind=kCustom, calls=%fused_computation | custom fusion | bytes 4210688 | tf_op jit(solution)/shard_map/gather | solution.py:66
  307.4 7.0 %convolution_bitcast_fusion = f32[512,256]{0,1:T(8,128)S(1)} fusion(bf16[8192,256]{1,0:T(8,128)(2,1)} %bitcast.38, bf16[512,8192]{1,0:T(8,128)(2,1)} %all-gather.2.cloned.1.call-done), kind=kOutput, calls=%fused_computation.11 | convolution fusion | flops 2147483648 | bytes 13107200 | tf_op jit(solution)/shard_map/dot_general | solution.py:68
  316.8 2.6 fusion.14
  319.4 3.5 reshape.39
  323.0 77.4 %all-reduce.1 = bf16[512,512]{1,0:T(8,128)(2,1)S(1)} all-reduce(f32[512,512]{1,0:T(8,128)S(1)} %reshape.39), channel_id=1, replica_groups=mesh['groups'=2,'fsdp'=8,'seq'=2] {'fsdp'}, use_global_device_ids=true, to_apply=%region_4.0 | all-reduce | flops 262144 | bytes 1572864 | tf_op jit(solution)/shard_map/psum | solution.py:97
  401.6 3.4 psum.15
  404.9 4.2 fusion.15
  409.1 62.2 %reduce-scatter.2.cloned.1.call-done = f32[16,1024]{1,0:T(8,128)} async-done(((f32[16,8192]{1,0:T(8,128)}), f32[16,1024]{1,0:T(8,128)}) %reduce-scatter.2.cloned.1.call-update) | async-done | bytes 65552 | tf_op jit(solution)/shard_map/reduce_scatter | solution.py:110
  (56 shorter events, 28.0 us)
Async XLA Ops:
  6.5 300.9 %all-gather.2.cloned.1.call-start = ((), (), s32[]{:S(2)}) async-start(), calls=%async_computation.2 | async-start | bytes 9437184 | tf_op jit(solution)/shard_map/all_gather | solution.py:69
  13.3 6.9 %copy-start.4 = (s32[160]{0:T(256)S(1)}, s32[160]{0:T(256)}, u32[]{:S(2)}) copy-start(s32[160]{0:T(256)} %param.12) | copy-start | bytes 1924
  66.3 218.2 %all-to-all-start = ((bf16[1024,8,256]{0,2,1:T(8,128)(2,1)}), bf16[1024,8,256]{0,2,1:T(8,128)(2,1)}, u32[]{:S(2)}, u32[]{:S(2)}) async-start(bf16[1024,8,256]{0,2,1:T(8,128)(2,1)} %all_to_all.14), calls=%async_computation | async-start | bytes 8388608 | tf_op jit(solution)/shard_map/all_to_all | solution.py:65
  73.8 397.5 %reduce-scatter.2.cloned.1.call-start = ((), (), s32[]{:S(2)}) async-start(), calls=%async_computation.3 | async-start | bytes 589824 | tf_op jit(solution)/shard_map/reduce_scatter | solution.py:110
  99.5 10.2 %copy-start.1 = (bf16[32,1024]{1,0:T(8,128)(2,1)S(1)}, bf16[32,1024]{1,0:T(8,128)(2,1)}, u32[]{:S(2)}) copy-start(bf16[32,1024]{1,0:T(8,128)(2,1)} %param.17) | copy-start | bytes 196612
  99.5 171.2 %copy-start.3 = (s32[16,256]{1,0:T(8,128)S(1)}, s32[16,256]{1,0:T(8,128)}, u32[]{:S(2)}) copy-start(s32[16,256]{1,0:T(8,128)} %param.18) | copy-start | bytes 49156
  100.5 1.3 copy-start
  101.9 168.9 %collective-permute-start = (bf16[128,1024]{1,0:T(8,128)(2,1)}, bf16[128,1024]{1,0:T(8,128)(2,1)S(1)}, u32[]{:S(2)}, u32[]{:S(2)}) collective-permute-start(bf16[128,1024]{1,0:T(8,128)(2,1)} %get-tuple-element.13), channel_id=1, source_target_pairs={{0,2},{2,0},{4,6},{6,4},{8,10},{10,8},{12,14},{14,12},{1,3},{3,1},... | collective-permute-start | bytes 786440 | tf_op jit(solution)/shard_map/ppermute | solution.py:23
  103.8 168.3 %collective-permute-start.1 = (bf16[128,1024]{1,0:T(8,128)(2,1)}, bf16[128,1024]{1,0:T(8,128)(2,1)S(1)}, u32[]{:S(2)}, u32[]{:S(2)}) collective-permute-start(bf16[128,1024]{1,0:T(8,128)(2,1)} %get-tuple-element.12), channel_id=1, source_target_pairs={{0,4},{2,6},{4,0},{6,2},{8,12},{10,14},{12,8},{14,10},{1,5},{3,7},... | collective-permute-start | bytes 786440 | tf_op jit(solution)/shard_map/ppermute | solution.py:23
  105.3 168.2 %collective-permute-start.2 = (bf16[128,1024]{1,0:T(8,128)(2,1)S(1)}, bf16[128,1024]{1,0:T(8,128)(2,1)S(1)}, u32[]{:S(2)}, u32[]{:S(2)}) collective-permute-start(bf16[128,1024]{1,0:T(8,128)(2,1)S(1)} %get-tuple-element.11), channel_id=1, source_target_pairs={{0,6},{2,4},{4,2},{6,0},{8,14},{10,12},{12,10},{14,8},{1,7},{3,5},... | collective-permute-start | bytes 786440 | tf_op jit(solution)/shard_map/ppermute | solution.py:23
  105.4 168.8 %collective-permute-start.3 = (bf16[128,1024]{1,0:T(8,128)(2,1)S(1)}, bf16[128,1024]{1,0:T(8,128)(2,1)S(1)}, u32[]{:S(2)}, u32[]{:S(2)}) collective-permute-start(bf16[128,1024]{1,0:T(8,128)(2,1)S(1)} %get-tuple-element.10), channel_id=1, source_target_pairs={{0,8},{2,10},{4,12},{6,14},{8,0},{10,2},{12,4},{14,6},{1,9},{3,11}... | collective-permute-start | bytes 786440 | tf_op jit(solution)/shard_map/ppermute | solution.py:23
  108.2 166.7 %collective-permute-start.4 = (bf16[128,1024]{1,0:T(8,128)(2,1)S(1)}, bf16[128,1024]{1,0:T(8,128)(2,1)S(1)}, u32[]{:S(2)}, u32[]{:S(2)}) collective-permute-start(bf16[128,1024]{1,0:T(8,128)(2,1)S(1)} %get-tuple-element.9), channel_id=1, source_target_pairs={{0,10},{2,8},{4,14},{6,12},{8,2},{10,0},{12,6},{14,4},{1,11},{3,9}... | collective-permute-start | bytes 786440 | tf_op jit(solution)/shard_map/ppermute | solution.py:23
  270.8 8.2 %collective-permute-start.5 = (bf16[128,1024]{1,0:T(8,128)(2,1)S(1)}, bf16[128,1024]{1,0:T(8,128)(2,1)S(1)}, u32[]{:S(2)}, u32[]{:S(2)}) collective-permute-start(bf16[128,1024]{1,0:T(8,128)(2,1)S(1)} %get-tuple-element.8), channel_id=1, source_target_pairs={{0,12},{2,14},{4,8},{6,10},{8,4},{10,6},{12,0},{14,2},{1,13},{3,15... | collective-permute-start | bytes 786440 | tf_op jit(solution)/shard_map/ppermute | solution.py:23
  272.1 9.2 %collective-permute-start.6 = (bf16[128,1024]{1,0:T(8,128)(2,1)S(1)}, bf16[128,1024]{1,0:T(8,128)(2,1)S(1)}, u32[]{:S(2)}, u32[]{:S(2)}) collective-permute-start(bf16[128,1024]{1,0:T(8,128)(2,1)S(1)} %get-tuple-element.7), channel_id=1, source_target_pairs={{0,14},{2,12},{4,10},{6,8},{8,6},{10,4},{12,2},{14,0},{1,15},{3,13... | collective-permute-start | bytes 786440 | tf_op jit(solution)/shard_map/ppermute | solution.py:23
  290.9 15.7 %copy-start.2 = (f32[16,256]{1,0:T(8,128)S(1)}, f32[16,256]{1,0:T(8,128)}, u32[]{:S(2)}) copy-start(f32[16,256]{1,0:T(8,128)} %param.19) | copy-start | bytes 49156
Sparse Core Ops, SparseCore 0:
  9.5 201.5 all-gather.1
  409.3 62.0 reduce-scatter.1
